TPU v7x, 32 devices: a whole 2x2x4 slice. The times are simulated.
32 devices in a mesh: grp: 8 (over y, x, core), head: 4 (over z).
Axes of the slice: x: 2, y: 2, z: 4, core: 2. Of those that a mesh axis runs over, the one named last changes fastest.
Arguments:
- q_nope: bfloat16 [4, 64, 128, 128], P(None, 'grp', 'head'), may hold values from -6 to 6
- q_rope: bfloat16 [4, 64, 128, 64], P(None, 'grp', 'head'), may hold values from -512 to 512
- w_absorb_k: bfloat16 [128, 128, 512], P('head'), may hold values from -0.5 to 0.5
- w_absorb_v: bfloat16 [128, 512, 128], P('head'), may hold values from -0.25 to 0.25
- latent_cache: bfloat16 [64, 1024, 576], P(('grp', 'head')), may hold values from -4 to 4
- new_latent: bfloat16 [4, 64, 576], P(None, ('grp', 'head')), may hold values from -6 to 6
- lengths: int32 [64], replicated, may hold values from 128 to 1020, as said below
- moves: int32 [4, 1], P('head'), may hold values from 1 to 7
Outputs:
- attended: bfloat16 [4, 64, 128, 128], P(None, 'grp', 'head')
Inputs may be any that keep to these rules, and one draw needn't show every extreme that they name: lengths[r] counts the live rows of latent_cache[r]; its later rows up to 1024 are padding that no query reads.
All inputs are finite; a program needn't handle non-finite values.
Results may differ from a plain program's by a relative error of at most 0.0077.
Values may be sent and summed in bfloat16 or wider, within the bound.
A program may use at most 64 MiB of HBM per device.

v0:
```python
import math

import jax
import jax.numpy as jnp
from jax import lax
from jax.sharding import PartitionSpec as P

HEAD_DIM = 128
ROPE = 64
LATENT = 512
BLOCK = 128


yarn_gain = (0.1 * math.log(40.0) + 1.0) ** 2


def passed_along(value, axis, steps):
    count = lax.axis_size(axis)
    pairs = [(source, (source + steps) % count) for source in range(count)]
    return lax.ppermute(value, axis, pairs)


def attend(queries, stored, counts, recent, moment, window, score_scale):
    holders = queries.shape[0]
    head_count = queries.shape[1]
    capacity = stored.shape[1]
    longest = jnp.max(counts)
    passes = (longest + window - 1) // window
    positions = jnp.arange(window, dtype=jnp.int32)

    def score_tile(tile_index, buffer):
        begin_at = tile_index * window
        key_rows = lax.dynamic_slice_in_dim(stored, begin_at, window, 1)
        partial_value = (
            jnp.einsum("rhc,rtc->rht", queries, key_rows, preferred_element_type=jnp.float32)
            * score_scale
        )
        inside = (begin_at + positions)[None, None, :] < counts[:, None, None]
        partial_value = jnp.where(inside, partial_value, -jnp.inf)
        return lax.dynamic_update_slice_in_dim(buffer, partial_value, begin_at, 2)

    empty = jnp.full((holders, head_count, capacity), -jnp.inf, jnp.float32)
    scores = lax.fori_loop(0, passes, score_tile, empty)
    extra_scores = (
        jnp.einsum("rhc,rjc->rhj", queries, recent, preferred_element_type=jnp.float32)
        * score_scale
    )
    step_live = jnp.arange(recent.shape[1], dtype=jnp.int32) <= moment
    extra_scores = jnp.where(step_live[None, None, :], extra_scores, -jnp.inf)
    peak = jnp.maximum(jnp.max(scores, axis=2), jnp.max(extra_scores, axis=2))[:, :, None]
    spread = jnp.exp(scores - peak)
    spread_new = jnp.exp(extra_scores - peak)
    softmax_sum = jnp.sum(spread, axis=2, keepdims=True) + jnp.sum(
        spread_new, axis=2, keepdims=True
    )
    weights = (spread / softmax_sum).astype(jnp.bfloat16)
    weights_new = (spread_new / softmax_sum).astype(jnp.bfloat16)
    start_value = jnp.einsum(
        "rhj,rjl->rhl", weights_new, recent[:, :, :LATENT], preferred_element_type=jnp.float32
    )

    def value_tile(tile_index, summed):
        begin_at = tile_index * window
        key_rows = lax.dynamic_slice_in_dim(stored, begin_at, window, 1)[:, :, :LATENT]
        weight_tile = lax.dynamic_slice_in_dim(weights, begin_at, window, 2)
        return summed + jnp.einsum(
            "rht,rtl->rhl", weight_tile, key_rows, preferred_element_type=jnp.float32
        )

    return lax.fori_loop(0, passes, value_tile, start_value).astype(jnp.bfloat16)


def body(q_nope, q_rope, w_absorb_k, w_absorb_v, latent_cache, new_latent, lengths, moves):
    step_count = q_nope.shape[0]
    holders = latent_cache.shape[0]
    capacity = latent_cache.shape[1]
    entries = latent_cache.shape[2]
    movers = moves.shape[1]
    window = min(4 * BLOCK, capacity)
    score_scale = yarn_gain / math.sqrt(HEAD_DIM + ROPE)
    group_count = lax.axis_size("grp")
    column_count = lax.axis_size("head")
    bit_count = group_count.bit_length() - 1
    offsets = moves[0]
    group_here = lax.axis_index("grp")
    column_here = lax.axis_index("head")
    first_slot = (group_here * column_count + column_here) * holders
    counts = lax.dynamic_slice_in_dim(lengths, first_slot, holders)
    source = jnp.mod(group_here - offsets, group_count)
    moved_counts = lengths[
        (source * column_count + column_here) * holders + jnp.arange(movers, dtype=jnp.int32)
    ]
    stored = latent_cache
    recent = jnp.zeros((holders, step_count, entries), jnp.bfloat16)
    results = []
    for moment in range(step_count):
        if moment == 2:
            moving = (stored[:movers], recent[:movers])
            for level in range(bit_count):
                arrived = passed_along((moving[0], moving[1]), "grp", 1 << level)
                chosen = offsets >> level & 1 == 1
                moving = (
                    jnp.where(chosen[:, None, None], arrived[0], moving[0]),
                    jnp.where(chosen[:, None, None], arrived[1], moving[1]),
                )
            stored = jnp.concatenate([moving[0], stored[movers:]], axis=0)
            recent = jnp.concatenate([moving[1], recent[movers:]], axis=0)
            counts = jnp.concatenate([moved_counts, counts[movers:]], axis=0)
        q_latent = jnp.einsum(
            "rhd,hdl->rhl", q_nope[moment], w_absorb_k, preferred_element_type=jnp.float32
        ).astype(jnp.bfloat16)
        query_rows = jnp.concatenate([q_latent, q_rope[moment]], axis=2)
        owned_rows = lax.all_to_all(query_rows, "head", split_axis=0, concat_axis=1, tiled=True)
        fresh_rows = new_latent[moment]
        recent = recent.at[:, moment].set(fresh_rows)
        latent_out = attend(owned_rows, stored, counts, recent, moment, window, score_scale)
        gathered = lax.all_to_all(latent_out, "head", split_axis=1, concat_axis=0, tiled=True)
        results.append(
            jnp.einsum(
                "rhl,hld->rhd", gathered, w_absorb_v, preferred_element_type=jnp.float32
            ).astype(jnp.bfloat16)
        )
    return jnp.stack(results)


def solution(mesh):
    placed = (
        P(None, "grp", "head", None),
        P(None, "grp", "head", None),
        P("head", None, None),
        P("head", None, None),
        P(("grp", "head"), None, None),
        P(None, ("grp", "head"), None),
        P(),
        P("head", None),
    )
    return jax.shard_map(
        body, mesh=mesh, in_specs=placed, out_specs=P(None, "grp", "head", None), check_vma=False
    )
```

profile of v0, /device:TPU:0, one launch (start us, length us, event | category | flops | bytes accessed | tf_op | source)
XLA Modules:
  0.0 186.6 jit_solution(15612328909421631202)
XLA Ops:
  6.6 2.8 %fusion.41 = bf16[8,32,512]{2,0,1:T(8,128)(2,1)S(1)} fusion(bf16[32,128,512]{2,1,0:T(8,128)(2,1)} %param.34, bf16[1,8,32,128]{3,2,1,0:T(8,128)(2,1)S(1)} %get-tuple-element.598), kind=kOutput, calls=%fused_computation.61 | convolution fusion | flops 33685504 | bytes 4521984 | tf_op jit(solution)/shard_map/rhd,hdl->rhl/dot_general | solution.py:109
  10.2 4.9 %all-to-all-start.2 = ((bf16[8,32,576]{2,1,0:T(8,128)(2,1)}), bf16[8,32,576]{2,1,0:T(8,128)(2,1)S(1)}, u32[]{:S(2)}, u32[]{:S(2)}) async-start(bf16[8,32,576]{2,1,0:T(8,128)(2,1)} %copy.84), calls=%async_computation.2 | async-start | bytes 655360 | tf_op jit(solution)/shard_map/all_to_all | solution.py:113
  15.6 2.8 %fusion.42 = bf16[8,32,512]{2,0,1:T(8,128)(2,1)S(1)} fusion(bf16[32,128,512]{2,1,0:T(8,128)(2,1)} %param.34, bf16[1,8,32,128]{3,2,1,0:T(8,128)(2,1)S(1)} %get-tuple-element.597), kind=kOutput, calls=%fused_computation.62 | convolution fusion | flops 33685504 | bytes 4521984 | tf_op jit(solution)/shard_map/rhd,hdl->rhl/dot_general | solution.py:109
  18.5 3.0 %fusion.43 = bf16[8,32,512]{2,0,1:T(8,128)(2,1)S(1)} fusion(bf16[32,128,512]{2,1,0:T(8,128)(2,1)} %param.34, bf16[1,8,32,128]{3,2,1,0:T(8,128)(2,1)S(1)} %get-tuple-element.599), kind=kOutput, calls=%fused_computation.63 | convolution fusion | flops 33685504 | bytes 4521984 | tf_op jit(solution)/shard_map/rhd,hdl->rhl/dot_general | solution.py:109
  31.5 3.1 %copy.79 = bf16[2,1024,576]{2,1,0:T(8,128)(2,1)S(1)} copy(bf16[2,1024,576]{1,2,0:T(8,128)(2,1)} %param.36) | data formatting | bytes 4718592 | tf_op jit(solution)/shard_map/while | solution.py:70
  39.5 5.1 %all-to-all-start = ((bf16[8,32,576]{2,1,0:T(8,128)(2,1)}), bf16[8,32,576]{2,1,0:T(8,128)(2,1)}, u32[]{:S(2)}, u32[]{:S(2)}) async-start(bf16[8,32,576]{2,1,0:T(8,128)(2,1)} %copy.73), calls=%async_computation | async-start | bytes 655360 | tf_op jit(solution)/shard_map/all_to_all | solution.py:113
  45.9 5.7 %while.94 = (s32[]{:T(128)}, f32[2,128,1024]{1,2,0:T(8,128)}, s32[]{:T(128)}, s32[2]{0:T(128)S(1)}, bf16[2,1024,576]{1,2,0:T(8,128)(2,1)}, /*index=5*/bf16[2,128...) while((s32[]{:T(128)}, f32[2,128,1024]{1,2,0:T(8,128)}, s32[]{:T(128)}, ...), condition=%wide.region_10.11_spmd.clone, body=%wide.region_9.10_spmd.clone.sunk | while | flops 151258624 | bytes 2006183 | solution.py:43
  46.0 2.8 %fusion.143 = f32[2,128,1024]{1,2,0:T(8,128)} fusion(f32[2,128,1024]{1,2,0:T(8,128)} %get-tuple-element.1027, s32[]{:T(128)S(6)} %select_n.188, bf16[2,128,576]{1,2,0:T(8,128)(2,1)S(1)} %get-tuple-element.1041, bf16[2,1024,576]{1,2,0:T(8,128)(2,1)} %get-tuple-element.1040, pred[2,512]{1,0:T(4,128)(4,1)S(1)} %broadcast_compare_fusion.9), kind=kOutput, calls=%fused_computation.31.clone.1 | convolution fusion | flops 151257088 | bytes 2000896 | tf_op jit(solution)/shard_map/while/body/rhc,rtc->rht/dot_general | solution.py:35
  48.8 2.8 %fusion.143 = f32[2,128,1024]{1,2,0:T(8,128)} fusion(f32[2,128,1024]{1,2,0:T(8,128)} %get-tuple-element.1027, s32[]{:T(128)S(6)} %select_n.188, bf16[2,128,576]{1,2,0:T(8,128)(2,1)S(1)} %get-tuple-element.1041, bf16[2,1024,576]{1,2,0:T(8,128)(2,1)} %get-tuple-element.1040, pred[2,512]{1,0:T(4,128)(4,1)S(1)} %broadcast_compare_fusion.9), kind=kOutput, calls=%fused_computation.31.clone.1 | convolution fusion | flops 151257088 | bytes 2000896 | tf_op jit(solution)/shard_map/while/body/rhc,rtc->rht/dot_general | solution.py:35
  54.0 3.5 %all-to-all-start.4 = ((bf16[8,32,576]{2,1,0:T(8,128)(2,1)}), bf16[8,32,576]{2,1,0:T(8,128)(2,1)S(1)}, u32[]{:S(2)}, u32[]{:S(2)}) async-start(bf16[8,32,576]{2,1,0:T(8,128)(2,1)} %copy.95), calls=%async_computation.4 | async-start | bytes 655360 | tf_op jit(solution)/shard_map/all_to_all | solution.py:113
  60.5 5.8 %while.93 = (s32[]{:T(128)}, f32[2,128,1024]{1,2,0:T(8,128)}, s32[]{:T(128)}, s32[2]{0:T(128)S(1)}, bf16[2,1024,576]{1,2,0:T(8,128)(2,1)}, /*index=5*/bf16[2,128...) while((s32[]{:T(128)}, f32[2,128,1024]{1,2,0:T(8,128)}, s32[]{:T(128)}, ...), condition=%wide.region_2.3_spmd.clone, body=%wide.region_1.2_spmd.clone.sunk | while | flops 151258624 | bytes 2006183 | solution.py:43
  60.5 2.8 %fusion.140 = f32[2,128,1024]{1,2,0:T(8,128)} fusion(f32[2,128,1024]{1,2,0:T(8,128)} %get-tuple-element.1084, s32[]{:T(128)S(6)} %select_n.186, bf16[2,128,576]{1,2,0:T(8,128)(2,1)} %get-tuple-element.1098, bf16[2,1024,576]{1,2,0:T(8,128)(2,1)} %get-tuple-element.1097, pred[2,512]{1,0:T(4,128)(4,1)S(1)} %broadcast_compare_fusion.8), kind=kOutput, calls=%fused_computation.23.clone.1 | convolution fusion | flops 151257088 | bytes 2000896 | tf_op jit(solution)/shard_map/while/body/rhc,rtc->rht/dot_general | solution.py:35
  63.5 2.8 %fusion.140 = f32[2,128,1024]{1,2,0:T(8,128)} fusion(f32[2,128,1024]{1,2,0:T(8,128)} %get-tuple-element.1084, s32[]{:T(128)S(6)} %select_n.186, bf16[2,128,576]{1,2,0:T(8,128)(2,1)} %get-tuple-element.1098, bf16[2,1024,576]{1,2,0:T(8,128)(2,1)} %get-tuple-element.1097, pred[2,512]{1,0:T(4,128)(4,1)S(1)} %broadcast_compare_fusion.8), kind=kOutput, calls=%fused_computation.23.clone.1 | convolution fusion | flops 151257088 | bytes 2000896 | tf_op jit(solution)/shard_map/while/body/rhc,rtc->rht/dot_general | solution.py:35
  73.4 2.7 %while.90 = (s32[]{:T(128)}, f32[2,128,512]{2,1,0:T(8,128)S(1)}, s32[]{:T(128)}, bf16[2,128,1024]{1,2,0:T(8,128)(2,1)}, bf16[2,1024,576]{2,1,0:T(8,128)(2,1)S(1)...) while((s32[]{:T(128)}, f32[2,128,512]{2,1,0:T(8,128)S(1)}, s32[]{:T(128)}, ...), condition=%wide.region_16.17_spmd, body=%wide.region_15.16_spmd.sunk | while | flops 134348800 | bytes 2360467 | solution.py:70
  82.3 6.5 %all-to-all-start.6 = ((bf16[8,32,576]{2,1,0:T(8,128)(2,1)}), bf16[8,32,576]{2,1,0:T(8,128)(2,1)}, u32[]{:S(2)}, u32[]{:S(2)}) async-start(bf16[8,32,576]{2,1,0:T(8,128)(2,1)} %copy.106), calls=%async_computation.6 | async-start | bytes 655360 | tf_op jit(solution)/shard_map/all_to_all | solution.py:113
  89.1 11.1 %collective-permute-done.4 = bf16[1,1024,576]{1,2,0:T(8,128)(2,1)} collective-permute-done((bf16[1,1024,576]{1,2,0:T(8,128)(2,1)}, bf16[1,1024,576]{1,2,0:T(8,128)(2,1)}, u32[]{:S(2)}, u32[]{:S(2)}) %collective-permute-start.4) | collective-permute-done | bytes 1179680 | tf_op jit(solution)/shard_map/ppermute | solution.py:20
  102.6 6.9 %all-to-all-start.3 = ((bf16[2,128,512]{2,0,1:T(2,128)(2,1)}), bf16[2,128,512]{2,0,1:T(2,128)(2,1)}, u32[]{:S(2)}, u32[]{:S(2)}) async-start(bf16[2,128,512]{2,0,1:T(2,128)(2,1)} %copy.154), calls=%async_computation.3 | async-start | bytes 524288 | tf_op jit(solution)/shard_map/all_to_all | solution.py:117
  109.5 2.7 %while.89 = (s32[]{:T(128)}, f32[2,128,512]{2,1,0:T(8,128)S(1)}, s32[]{:T(128)}, bf16[2,128,1024]{1,2,0:T(8,128)(2,1)}, bf16[2,1024,576]{2,1,0:T(8,128)(2,1)S(1)...) while((s32[]{:T(128)}, f32[2,128,512]{2,1,0:T(8,128)S(1)}, s32[]{:T(128)}, ...), condition=%wide.region_8.9_spmd, body=%wide.region_7.8_spmd.sunk | while | flops 134348800 | bytes 2360467 | solution.py:70
  113.3 3.2 %all-to-all-done.3 = bf16[2,128,512]{2,0,1:T(2,128)(2,1)} async-done(((bf16[2,128,512]{2,0,1:T(2,128)(2,1)}), bf16[2,128,512]{2,0,1:T(2,128)(2,1)}, u32[]{:S(2)}, u32[]{:S(2)}) %all-to-all-start.3) | async-done | bytes 262176 | tf_op jit(solution)/shard_map/all_to_all | solution.py:117
  116.5 3.4 %all-to-all-start.1 = ((bf16[2,128,512]{2,0,1:T(2,128)(2,1)}), bf16[2,128,512]{2,0,1:T(2,128)(2,1)S(1)}, u32[]{:S(2)}, u32[]{:S(2)}) async-start(bf16[2,128,512]{2,0,1:T(2,128)(2,1)} %copy.155), calls=%async_computation.1 | async-start | bytes 524288 | tf_op jit(solution)/shard_map/all_to_all | solution.py:117
  127.6 2.8 %fusion.45 = bf16[1,8,32,128]{3,1,2,0:T(8,128)(2,1)S(1)} fusion(bf16[8,32,512]{2,0,1:T(8,128)(2,1)S(1)} %all_to_all.119, bf16[32,512,128]{2,1,0:T(8,128)(2,1)} %param.35), kind=kOutput, calls=%fused_computation.69 | convolution fusion | flops 33587200 | bytes 4521984 | tf_op jit(solution)/shard_map/rhl,hld->rhd/dot_general | solution.py:119
  132.4 3.5 %while.95 = (s32[]{:T(128)}, f32[2,128,1024]{1,2,0:T(8,128)S(1)}, s32[]{:T(128)}, s32[2]{0:T(128)S(1)}, bf16[2,1024,576]{1,2,0:T(8,128)(2,1)S(1)}, /*index=5*/bf...) while((s32[]{:T(128)}, f32[2,128,1024]{1,2,0:T(8,128)S(1)}, ...), condition=%wide.region_18.19_spmd.clone, body=%wide.region_17.18_spmd.clone.sunk | while | flops 151258624 | bytes 2007207 | solution.py:43
  138.0 4.2 %while.96 = (s32[]{:T(128)}, f32[2,128,1024]{1,2,0:T(8,128)S(1)}, s32[]{:T(128)}, s32[2]{0:T(128)S(1)}, bf16[2,1024,576]{1,2,0:T(8,128)(2,1)}, /*index=5*/bf16[2...) while((s32[]{:T(128)}, f32[2,128,1024]{1,2,0:T(8,128)S(1)}, s32[]{:T(128)}, ...), condition=%wide.region_26.27_spmd.clone, body=%wide.region_25.26_spmd.clone.sunk | while | flops 151258624 | bytes 2007207 | solution.py:43
  145.0 3.1 %copy.101 = bf16[2,1024,576]{2,1,0:T(8,128)(2,1)S(1)} copy(bf16[2,1024,576]{1,2,0:T(8,128)(2,1)} %get-tuple-element.1135) | data formatting | bytes 4718592 | tf_op jit(solution)/shard_map/while | solution.py:70
  150.3 4.5 %while.92 = (s32[]{:T(128)}, f32[2,128,512]{2,1,0:T(8,128)}, s32[]{:T(128)}, bf16[2,128,1024]{1,2,0:T(8,128)(2,1)}, bf16[2,1024,576]{2,1,0:T(8,128)(2,1)S(1)}, /*index=5*/s32[]{:T(128)}, s32[]{:T(128)}, s32[]{:T(128)}, s32[]{:T(128)}) while((s32[]{:T(128)}, f32[2,128,512]{2,1,0:T(8,128)}, s32[]{:T(128)}, bf16[2,128,1024]{1,2,0:T(8,128)(2,1)}, ...), condition=%wide.region_32.33_spmd, body=%wide.region_31.32_spmd.sunk | while | flops 134348800 | bytes 2360467 | solution.py:70
  157.0 4.0 %all-to-all-start.7 = ((bf16[2,128,512]{2,0,1:T(2,128)(2,1)}), bf16[2,128,512]{2,0,1:T(2,128)(2,1)}, u32[]{:S(2)}, u32[]{:S(2)}) async-start(bf16[2,128,512]{2,0,1:T(2,128)(2,1)} %copy.152), calls=%async_computation.7 | async-start | bytes 524288 | tf_op jit(solution)/shard_map/all_to_all | solution.py:117
  161.0 2.7 %while.91 = (s32[]{:T(128)}, f32[2,128,512]{2,1,0:T(8,128)S(1)}, s32[]{:T(128)}, bf16[2,128,1024]{1,2,0:T(8,128)(2,1)}, bf16[2,1024,576]{2,1,0:T(8,128)(2,1)S(1)...) while((s32[]{:T(128)}, f32[2,128,512]{2,1,0:T(8,128)S(1)}, s32[]{:T(128)}, ...), condition=%wide.region_24.25_spmd, body=%wide.region_23.24_spmd.sunk | while | flops 134348800 | bytes 2360467 | solution.py:70
  164.9 5.6 %all-to-all-done.7 = bf16[2,128,512]{2,0,1:T(2,128)(2,1)} async-done(((bf16[2,128,512]{2,0,1:T(2,128)(2,1)}), bf16[2,128,512]{2,0,1:T(2,128)(2,1)}, u32[]{:S(2)}, u32[]{:S(2)}) %all-to-all-start.7) | async-done | bytes 262176 | tf_op jit(solution)/shard_map/all_to_all | solution.py:117
  170.4 3.4 %all-to-all-start.5 = ((bf16[2,128,512]{2,0,1:T(2,128)(2,1)}), bf16[2,128,512]{2,0,1:T(2,128)(2,1)S(1)}, u32[]{:S(2)}, u32[]{:S(2)}) async-start(bf16[2,128,512]{2,0,1:T(2,128)(2,1)} %copy.153), calls=%async_computation.5 | async-start | bytes 524288 | tf_op jit(solution)/shard_map/all_to_all | solution.py:117
  173.9 2.8 %fusion.44 = bf16[1,8,32,128]{3,1,2,0:T(8,128)(2,1)S(1)} fusion(bf16[8,32,512]{2,0,1:T(8,128)(2,1)S(1)} %copy-done.11, bf16[32,512,128]{2,1,0:T(8,128)(2,1)} %param.35), kind=kOutput, calls=%fused_computation.68 | convolution fusion | flops 33587200 | bytes 4521984 | tf_op jit(solution)/shard_map/rhl,hld->rhd/dot_general | solution.py:119
  178.0 2.8 %fusion.47 = bf16[1,8,32,128]{3,1,2,0:T(8,128)(2,1)S(1)} fusion(bf16[8,32,512]{2,0,1:T(8,128)(2,1)S(1)} %all_to_all.135, bf16[32,512,128]{2,1,0:T(8,128)(2,1)} %param.35), kind=kOutput, calls=%fused_computation.71 | convolution fusion | flops 33587200 | bytes 4521984 | tf_op jit(solution)/shard_map/rhl,hld->rhd/dot_general | solution.py:119
  183.0 2.8 %fusion.46 = bf16[1,8,32,128]{3,1,2,0:T(8,128)(2,1)S(1)} fusion(bf16[8,32,512]{2,0,1:T(8,128)(2,1)S(1)} %all_to_all.127, bf16[32,512,128]{2,1,0:T(8,128)(2,1)} %param.35), kind=kOutput, calls=%fused_computation.70 | convolution fusion | flops 33587200 | bytes 4521984 | tf_op jit(solution)/shard_map/rhl,hld->rhd/dot_general | solution.py:119
  (175 shorter events, 88.4 us)
Async XLA Ops:
  0.0 6.4 %copy-start.12 = (bf16[4,8,32,64]{3,2,1,0:T(8,128)(2,1)S(1)}, bf16[4,8,32,64]{3,2,1,0:T(8,128)(2,1)}, u32[]{:S(2)}) copy-start(bf16[4,8,32,64]{3,2,1,0:T(8,128)(2,1)} %param.33) | copy-start | bytes 393220
  0.0 6.5 %copy-start.13 = (bf16[4,8,32,128]{3,2,1,0:T(8,128)(2,1)S(1)}, bf16[4,8,32,128]{3,2,1,0:T(8,128)(2,1)}, u32[]{:S(2)}) copy-start(bf16[4,8,32,128]{3,2,1,0:T(8,128)(2,1)} %param.32) | copy-start | bytes 786436
  0.9 26.0 %collective-permute-start = (bf16[1,4,576]{2,1,0:T(4,128)(2,1)S(1)}, bf16[1,4,576]{2,1,0:T(4,128)(2,1)S(1)}, u32[]{:S(2)}, u32[]{:S(2)}) collective-permute-start(bf16[1,4,576]{2,1,0:T(4,128)(2,1)S(1)} %slice.181), channel_id=1, source_target_pairs={{0,4},{4,8},{8,12},{12,16},{16,20},{20,24},{24,28},{28,0},{1,5},{5... | collective-permute-start | bytes 13832 | tf_op jit(solution)/shard_map/ppermute | solution.py:20
  3.8 67.9 %collective-permute-start.3 = (bf16[1,1024,576]{1,2,0:T(8,128)(2,1)}, bf16[1,1024,576]{1,2,0:T(8,128)(2,1)}, u32[]{:S(2)}, u32[]{:S(2)}) collective-permute-start(bf16[1,1024,576]{1,2,0:T(8,128)(2,1)} %slice.168), channel_id=1, source_target_pairs={{0,4},{4,8},{8,12},{12,16},{16,20},{20,24},{24,28},{28,0},{1,5},{5... | collective-permute-start | bytes 3538952 | tf_op jit(solution)/shard_map/ppermute | solution.py:20
  10.2 29.3 %all-to-all-start.2 = ((bf16[8,32,576]{2,1,0:T(8,128)(2,1)}), bf16[8,32,576]{2,1,0:T(8,128)(2,1)S(1)}, u32[]{:S(2)}, u32[]{:S(2)}) async-start(bf16[8,32,576]{2,1,0:T(8,128)(2,1)} %copy.84), calls=%async_computation.2 | async-start | bytes 655360 | tf_op jit(solution)/shard_map/all_to_all | solution.py:113
  18.5 3.5 %copy-start = (bf16[32,128,512]{2,1,0:T(8,128)(2,1)S(1)}, bf16[32,128,512]{2,1,0:T(8,128)(2,1)}, u32[]{:S(2)}) copy-start(bf16[32,128,512]{2,1,0:T(8,128)(2,1)} %param.34) | copy-start | bytes 12582916
  21.9 2.3 %copy-start.14 = (s32[64]{0:T(128)S(1)}, s32[64]{0:T(128)}, u32[]{:S(2)}) copy-start(s32[64]{0:T(128)} %param.38) | copy-start | bytes 772
  26.9 12.0 %collective-permute-start.1 = (bf16[1,4,576]{2,1,0:T(4,128)(2,1)S(1)}, bf16[1,4,576]{2,1,0:T(4,128)(2,1)S(1)}, u32[]{:S(2)}, u32[]{:S(2)}) collective-permute-start(bf16[1,4,576]{2,1,0:T(4,128)(2,1)S(1)} %get-tuple-element.608), channel_id=1, source_target_pairs={{0,8},{4,12},{8,16},{12,20},{16,24},{20,28},{24,0},{28,4},{1,9},{5... | collective-permute-start | bytes 13832 | tf_op jit(solution)/shard_map/ppermute | solution.py:20
  38.9 81.0 %collective-permute-start.2 = (bf16[1,4,576]{2,1,0:T(4,128)(2,1)S(1)}, bf16[1,4,576]{2,1,0:T(4,128)(2,1)S(1)}, u32[]{:S(2)}, u32[]{:S(2)}) collective-permute-start(bf16[1,4,576]{2,1,0:T(4,128)(2,1)S(1)} %broadcast_select_fusion.4), channel_id=1, source_target_pairs={{0,16},{4,20},{8,24},{12,28},{16,0},{20,4},{24,8},{28,12},{1,17},{... | collective-permute-start | bytes 13832 | tf_op jit(solution)/shard_map/ppermute | solution.py:20
  39.5 14.5 %all-to-all-start = ((bf16[8,32,576]{2,1,0:T(8,128)(2,1)}), bf16[8,32,576]{2,1,0:T(8,128)(2,1)}, u32[]{:S(2)}, u32[]{:S(2)}) async-start(bf16[8,32,576]{2,1,0:T(8,128)(2,1)} %copy.73), calls=%async_computation | async-start | bytes 655360 | tf_op jit(solution)/shard_map/all_to_all | solution.py:113
  44.6 1.3 copy-start.10
  54.0 28.3 %all-to-all-start.4 = ((bf16[8,32,576]{2,1,0:T(8,128)(2,1)}), bf16[8,32,576]{2,1,0:T(8,128)(2,1)S(1)}, u32[]{:S(2)}, u32[]{:S(2)}) async-start(bf16[8,32,576]{2,1,0:T(8,128)(2,1)} %copy.95), calls=%async_computation.4 | async-start | bytes 655360 | tf_op jit(solution)/shard_map/all_to_all | solution.py:113
  58.5 2.0 %copy-start.9 = (bf16[4,2,32,576]{3,2,0,1:T(8,128)(2,1)}, bf16[4,2,32,576]{3,2,0,1:T(8,128)(2,1)S(1)}, u32[]{:S(2)}) copy-start(bf16[4,2,32,576]{3,2,0,1:T(8,128)(2,1)S(1)} %copy.74) | copy-start | bytes 884740
  60.5 7.2 %copy-start.15 = (pred[4]{0:T(512)(128)(4,1)S(1)}, pred[4]{0:T(512)(128)(4,1)}, u32[]{:S(2)}) copy-start(pred[4]{0:T(512)(128)(4,1)} %iota_compare_fusion.2) | copy-start | bytes 16
  67.6 3.1 %copy-start.1 = (f32[2,128,1024]{1,2,0:T(8,128)S(1)}, f32[2,128,1024]{1,2,0:T(8,128)}, u32[]{:S(2)}) copy-start(f32[2,128,1024]{1,2,0:T(8,128)} %get-tuple-element.319) | copy-start | bytes 3145732
  67.7 4.1 %copy-start.4 = (bf16[2,1024,576]{1,2,0:T(8,128)(2,1)S(1)}, bf16[2,1024,576]{1,2,0:T(8,128)(2,1)}, u32[]{:S(2)}) copy-start(bf16[2,1024,576]{1,2,0:T(8,128)(2,1)} %get-tuple-element.1133) | copy-start | bytes 7077892
  73.4 26.8 %collective-permute-start.4 = (bf16[1,1024,576]{1,2,0:T(8,128)(2,1)}, bf16[1,1024,576]{1,2,0:T(8,128)(2,1)}, u32[]{:S(2)}, u32[]{:S(2)}) collective-permute-start(bf16[1,1024,576]{1,2,0:T(8,128)(2,1)} %get-tuple-element.594), channel_id=1, source_target_pairs={{0,8},{4,12},{8,16},{12,20},{16,24},{20,28},{24,0},{28,4},{1,9},{5... | collective-permute-start | bytes 3538952 | tf_op jit(solution)/shard_map/ppermute | solution.py:20
  77.5 3.8 %copy-start.2 = (f32[2,128,1024]{1,2,0:T(8,128)S(1)}, f32[2,128,1024]{1,2,0:T(8,128)}, u32[]{:S(2)}) copy-start(f32[2,128,1024]{1,2,0:T(8,128)} %get-tuple-element.317) | copy-start | bytes 3145732
  82.3 20.3 %all-to-all-start.6 = ((bf16[8,32,576]{2,1,0:T(8,128)(2,1)}), bf16[8,32,576]{2,1,0:T(8,128)(2,1)}, u32[]{:S(2)}, u32[]{:S(2)}) async-start(bf16[8,32,576]{2,1,0:T(8,128)(2,1)} %copy.106), calls=%async_computation.6 | async-start | bytes 655360 | tf_op jit(solution)/shard_map/all_to_all | solution.py:113
  102.6 27.9 %collective-permute-start.5 = (bf16[1,1024,576]{1,2,0:T(8,128)(2,1)}, bf16[1,1024,576]{1,2,0:T(8,128)(2,1)}, u32[]{:S(2)}, u32[]{:S(2)}) collective-permute-start(bf16[1,1024,576]{1,2,0:T(8,128)(2,1)} %broadcast_select_fusion.1), channel_id=1, source_target_pairs={{0,16},{4,20},{8,24},{12,28},{16,0},{20,4},{24,8},{28,12},{1,17},{... | collective-permute-start | bytes 3538952 | tf_op jit(solution)/shard_map/ppermute | solution.py:20
  102.6 13.9 %all-to-all-start.3 = ((bf16[2,128,512]{2,0,1:T(2,128)(2,1)}), bf16[2,128,512]{2,0,1:T(2,128)(2,1)}, u32[]{:S(2)}, u32[]{:S(2)}) async-start(bf16[2,128,512]{2,0,1:T(2,128)(2,1)} %copy.154), calls=%async_computation.3 | async-start | bytes 524288 | tf_op jit(solution)/shard_map/all_to_all | solution.py:117
  116.5 10.2 %all-to-all-start.1 = ((bf16[2,128,512]{2,0,1:T(2,128)(2,1)}), bf16[2,128,512]{2,0,1:T(2,128)(2,1)S(1)}, u32[]{:S(2)}, u32[]{:S(2)}) async-start(bf16[2,128,512]{2,0,1:T(2,128)(2,1)} %copy.155), calls=%async_computation.1 | async-start | bytes 524288 | tf_op jit(solution)/shard_map/all_to_all | solution.py:117
  122.1 8.4 %copy-start.7 = (bf16[4,2,32,576]{3,2,0,1:T(8,128)(2,1)}, bf16[4,2,32,576]{3,2,0,1:T(8,128)(2,1)S(1)}, u32[]{:S(2)}) copy-start(bf16[4,2,32,576]{3,2,0,1:T(8,128)(2,1)S(1)} %copy.107) | copy-start | bytes 884740
  130.5 1.6 copy-start.6
  135.9 1.0 copy-start.3
  136.0 1.7 copy-start.5
  138.0 4.3 %copy-start.8 = (bf16[4,2,32,576]{3,2,0,1:T(8,128)(2,1)S(1)}, bf16[4,2,32,576]{3,2,0,1:T(8,128)(2,1)}, u32[]{:S(2)}) copy-start(bf16[4,2,32,576]{3,2,0,1:T(8,128)(2,1)} %copy-done.7) | copy-start | bytes 884740
  157.0 13.5 %all-to-all-start.7 = ((bf16[2,128,512]{2,0,1:T(2,128)(2,1)}), bf16[2,128,512]{2,0,1:T(2,128)(2,1)}, u32[]{:S(2)}, u32[]{:S(2)}) async-start(bf16[2,128,512]{2,0,1:T(2,128)(2,1)} %copy.152), calls=%async_computation.7 | async-start | bytes 524288 | tf_op jit(solution)/shard_map/all_to_all | solution.py:117
  161.0 12.8 %copy-start.11 = (bf16[8,32,512]{2,0,1:T(8,128)(2,1)S(1)}, bf16[8,32,512]{2,0,1:T(8,128)(2,1)}, u32[]{:S(2)}) copy-start(bf16[8,32,512]{2,0,1:T(8,128)(2,1)} %all_to_all.111) | copy-start | bytes 786436
  170.4 12.2 %all-to-all-start.5 = ((bf16[2,128,512]{2,0,1:T(2,128)(2,1)}), bf16[2,128,512]{2,0,1:T(2,128)(2,1)S(1)}, u32[]{:S(2)}, u32[]{:S(2)}) async-start(bf16[2,128,512]{2,0,1:T(2,128)(2,1)} %copy.153), calls=%async_computation.5 | async-start | bytes 524288 | tf_op jit(solution)/shard_map/all_to_all | solution.py:117
where the time goes:
time: 187 us
  matrix products  56.6 us (30%)
  starting transfers between devices  42.9 us (23%)
  local copies, waits for them, and re-layouts  35.3 us (19%)
  waiting for transfers between devices  26.3 us (14%)
  other arithmetic  22.1 us (12%)
  between operations  3.07 us (2%)
    all_to_all x4, starting transfers between devices, body(): lax.all_to_all(query_rows, 'head', split_axis=0, concat_axis=1, tiled=True)  20 us
    dot_general x8, matrix products, score_tile(): jnp.einsum('rhc,rtc->rht', queries, key_rows, preferred_element_type=jnp....  18.5 us
    all_to_all x4, starting transfers between devices, body(): lax.all_to_all(latent_out, 'head', split_axis=1, concat_axis=0, tiled=True)  17.7 us
    all_to_all x4, waiting for transfers between devices, body(): lax.all_to_all(latent_out, 'head', split_axis=1, concat_axis=0, tiled=True)  12.7 us
    dot_general x8, matrix products, value_tile(): jnp.einsum('rht,rtl->rhl', weight_tile, key_rows, preferred_element_type=...  12.5 us
    while x6, local copies, waits for them, and re-layouts, attend(): lax.fori_loop(0, passes, value_tile, start_value).astype(jnp.bfloat16)  11.7 us
    dot_general x4, matrix products, body(): jnp.einsum('rhl,hld->rhd', gathered, w_absorb_v, preferred_element_type=j...  11.3 us
    ppermute x6, waiting for transfers between devices, passed_along(): return lax.ppermute(value, axis, pairs)  11.1 us
  transfers between devices with their start and end apart: 14, of which 6 were waited for; matrix products, arithmetic and copies ran while one was open for 44% of the time, Pallas kernels for 0%

commit v1 on v0

v1 whole, which is shorter than its diff:
```python
import functools
import math

import jax
import jax.numpy as jnp
from jax import lax
from jax.experimental import pallas as pl
from jax.experimental.pallas import tpu as pltpu
from jax.sharding import PartitionSpec as P

PAIR = 2
EXTRA = 128
LANES = 128
YARN_GAIN = (0.1 * math.log(40.0) + 1.0) ** 2
MESH = pl.DeviceIdType.MESH


def lane(c):
    return slice(c * LANES, (c + 1) * LANES)


def rounded(value):
    return value.astype(jnp.bfloat16)


def wide(value):
    return value.astype(jnp.float32)


def kernel(
    groups, columns, scale,
    length_ref, move_ref, nope_ref, rope_ref, fresh_ref, wk_hbm, wv_hbm, cache_hbm,
    out_ref,
    wk, wv, keys, local_sem,
    rows_in, rows_mid, rows_out,
    lat_send, lat_recv, rot_send, rot_recv, back_send, back_recv,
    mine, moved, mine_key, moved_key, home, home_recv, shift_of, shift_mine,
    lat_ss, lat_rs, rot_ss, rot_rs, back_ss, back_rs,
    mine_ss, mine_rs, key_ss, key_rs, home_ss, home_rs, shift_ss, shift_rs,
):
    steps, _, heads, _ = nope_ref.shape
    holders, capacity, entries = cache_hbm.shape
    latent = wk.shape[2]
    rope = entries - latent
    movers = move_ref.shape[1]
    spans = steps // PAIR
    total = capacity + EXTRA
    rank = lax.axis_index("grp")
    column = lax.axis_index("head")
    parts = wk.shape[0] // local_part(heads)
    part = local_part(heads)

    wk_copies = [
        pltpu.make_async_copy(
            wk_hbm.at[pl.ds(n * part, part)], wk.at[pl.ds(n * part, part)], local_sem.at[n]
        )
        for n in range(parts)
    ]
    key_copies = [
        pltpu.make_async_copy(
            cache_hbm.at[k], keys.at[k, pl.ds(0, capacity)], local_sem.at[parts + k]
        )
        for k in range(holders)
    ]
    wv_copy = pltpu.make_async_copy(wv_hbm, wv, local_sem.at[parts + holders])
    for copy in wk_copies:
        copy.start()

    def at_column(e):
        return (rank, lax.rem(column + e + columns, columns))

    def at_group(d):
        return (lax.rem(rank + d + groups, groups), column)

    def remote(src, dst, send, recv, target):
        return pltpu.make_async_remote_copy(
            src_ref=src, dst_ref=dst, send_sem=send, recv_sem=recv,
            device_id=target, device_id_type=MESH,
        )

    barrier = pltpu.get_barrier_semaphore()
    for e in range(1, columns):
        pl.semaphore_signal(barrier, inc=1, device_id=at_column(e), device_id_type=MESH)
    for d in range(1, groups):
        pl.semaphore_signal(barrier, inc=1, device_id=at_group(d), device_id_type=MESH)

    def slot(e, k):
        return lax.rem(column + e, columns) * holders + k

    def turned(span, e, k):
        return jnp.concatenate(
            [rope_ref[span * PAIR + s, slot(e, k)] for s in range(PAIR)], axis=1
        )

    for k in range(movers):
        for e in range(columns):
            for s in range(PAIR):
                mine[k, s, e] = nope_ref[PAIR + s, slot(e, k)]
            mine[k, PAIR, e] = turned(1, e, k)
        shift_mine[k] = jnp.full(shift_mine.shape[1:], move_ref[0, k], jnp.int32)
        shift_of[0, k] = jnp.full(shift_mine.shape[1:], move_ref[0, k], jnp.int32)
    row = lax.broadcasted_iota(jnp.int32, (16, entries), 0)

    def fresh_rows(k):
        found = jnp.zeros((16, entries), jnp.float32)
        for j in range(steps):
            found = jnp.where(row == j, wide(fresh_ref[j])[k : k + 1], found)
        return found

    for k in range(holders):
        keys[k, pl.ds(capacity, EXTRA)] = jnp.zeros((EXTRA, entries), jnp.bfloat16)
        keys[k, pl.ds(capacity, 16)] = rounded(fresh_rows(k))
    for k in range(movers):
        mine_key[k] = rounded(fresh_rows(k))
    pl.semaphore_wait(barrier, columns - 1 + groups - 1)

    shift_copies = [
        remote(shift_mine, shift_of.at[e], shift_ss.at[e], shift_rs.at[e], at_column(-e))
        for e in range(1, columns)
    ]
    mine_copies = [
        remote(mine, moved.at[d - 1], mine_ss.at[d - 1], mine_rs.at[d - 1], at_group(-d))
        for d in range(1, groups)
    ]
    newer_copies = [
        remote(mine_key, moved_key.at[d - 1], key_ss.at[d - 1], key_rs.at[d - 1], at_group(-d))
        for d in range(1, groups)
    ]
    for copy in shift_copies + mine_copies + newer_copies:
        copy.start()
    for copy in key_copies:
        copy.start()
    wv_copy.start()

    def lat_copy(u, e):
        return remote(
            lat_send.at[u, e], lat_recv.at[u, e], lat_ss.at[u, e], lat_rs.at[u, e], at_column(e)
        )

    def rot_copy(u, e):
        return remote(
            rot_send.at[u, e], rot_recv.at[u, e], rot_ss.at[u, e], rot_rs.at[u, e], at_column(e)
        )

    def back_copy(u, e):
        return remote(
            back_send.at[u, e], back_recv.at[u, e], back_ss.at[u, e], back_rs.at[u, e],
            at_column(-e),
        )

    def chosen(e, k, options):
        found = wide(options(0))
        for d in range(2, groups):
            is_it = shift_of[e, k, 0:1, 0:1] == d
            found = jnp.where(is_it, wide(options(d - 1)), found)
        return found

    count = holders * columns * PAIR
    unit_rows = columns * PAIR * heads

    def place(k, e, s):
        return ((k * columns + e) * PAIR + s) * heads

    def absorb(span, first):
        for k in range(holders):
            for e in range(columns):
                for s in range(PAIR):
                    if span and k < movers:
                        value = chosen(e, k, lambda n: moved[n, k, s, e])
                    else:
                        value = wide(nope_ref[span * PAIR + s, slot(e, k)])
                    rows_in[pl.ds(place(k, e, s), heads)] = value
                if span and k < movers:
                    pair = rounded(chosen(e, k, lambda n: moved[n, k, PAIR, e]))
                else:
                    pair = turned(span, e, k)
                if e:
                    rot_send[span * holders + k, e] = pair
                else:
                    rot_recv[span * holders + k, 0] = pair
        for n in range(parts):
            if first:
                wk_copies[n].wait()

            def head(i, carry):
                picked = rounded(rows_in[pl.ds(i, count, stride=heads)])
                result = jnp.dot(picked, wk[i], preferred_element_type=jnp.float32)
                for c in range(latent // LANES):
                    rows_mid[c, pl.ds(i, count, stride=heads)] = result[:, lane(c)]
                return carry

            lax.fori_loop(n * part, (n + 1) * part, head, 0)
        for k in range(holders):
            u = span * holders + k
            for e in range(columns):
                at = pl.ds(place(k, e, 0), PAIR * heads)
                value = jnp.concatenate(
                    [rounded(rows_mid[c, at]) for c in range(latent // LANES)], axis=1
                )
                if e:
                    lat_send[u, e] = value
                    lat_copy(u, e).start()
                    rot_copy(u, e).start()
                else:
                    lat_recv[u, 0] = value

    absorb(0, True)
    for copy in shift_copies:
        copy.wait()
    for copy in mine_copies + newer_copies:
        copy.wait()
    for span in range(1, spans):
        absorb(span, False)
    for copy in key_copies:
        copy.wait()
    for k in range(movers):
        later = chosen(0, k, lambda n: moved_key[n, k])
        keys[k, pl.ds(capacity, 16)] = rounded(
            jnp.where(row < PAIR, wide(keys[k, pl.ds(capacity, 16)]), later)
        )

    at_key = lax.broadcasted_iota(jnp.int32, (1, total), 1)
    at_row = lax.broadcasted_iota(jnp.int32, (unit_rows, 1), 0)
    within = lax.rem(lax.div(at_row, heads), PAIR)

    def unit(u, carry):
        span = lax.div(u, holders)
        k = lax.rem(u, holders)
        for e in range(1, columns):
            lat_copy(u, e).wait_recv()
            rot_copy(u, e).wait_recv()
        live = length_ref[(rank * columns + column) * holders + k]
        token = jnp.where(at_key < capacity, steps, at_key - capacity)
        token = jnp.where(at_key < live, -1, token)
        nt = (((1,), (1,)), ((), ()))
        queries = lat_recv[u].reshape(unit_rows, latent)
        turns = rot_recv[u]
        turns = jnp.concatenate(
            [turns[e][:, s * rope : (s + 1) * rope] for e in range(columns) for s in range(PAIR)],
            axis=0,
        )
        scores = lax.dot_general(
            queries, keys[k, :, :latent], nt, preferred_element_type=jnp.float32
        ) + lax.dot_general(
            turns, keys[k, :, latent:], nt, preferred_element_type=jnp.float32
        )
        scores = jnp.where(token <= span * PAIR + within, scores * scale, -jnp.inf)
        spread = jnp.exp(scores - jnp.max(scores, axis=1, keepdims=True))
        weights = rounded(spread / jnp.sum(spread, axis=1, keepdims=True))
        mixed = rounded(
            jnp.dot(weights, keys[k, :, :latent], preferred_element_type=jnp.float32)
        ).reshape(columns, PAIR * heads, latent)
        back_recv[u, 0] = mixed[0]
        for e in range(1, columns):
            back_send[u, e] = mixed[e]
            back_copy(u, e).start()
        return carry

    lax.fori_loop(0, spans * holders, unit, 0)
    wv_copy.wait()

    def project(span, members):
        held = len(members)
        for n, k in enumerate(members):
            u = span * holders + k
            for e in range(1, columns):
                back_copy(u, e).wait_recv()
            for e in range(columns):
                value = wide(back_recv[u, e])
                for c in range(latent // LANES):
                    rows_mid[c, pl.ds(place(n, e, 0), PAIR * heads)] = value[:, lane(c)]

        def head(i, carry):
            at = pl.ds(i, held * columns * PAIR, stride=heads)
            picked = jnp.concatenate(
                [rounded(rows_mid[c, at]) for c in range(latent // LANES)], axis=1
            )
            rows_out[pl.ds(i, held * columns * PAIR, stride=heads)] = jnp.dot(
                picked, wv[i], preferred_element_type=jnp.float32
            )
            return carry

        lax.fori_loop(0, heads, head, 0)
        for n, k in enumerate(members):
            for e in range(columns):
                for s in range(PAIR):
                    value = rounded(rows_out[pl.ds(place(n, e, s), heads)])
                    if span and k < movers:
                        home[k, s, e] = value
                    else:
                        out_ref[span * PAIR + s, slot(e, k)] = value

    home_copies = [
        remote(home, home_recv.at[d - 1], home_ss.at[d - 1], home_rs.at[d - 1], at_group(d))
        for d in range(1, groups)
    ]
    project(0, list(range(holders)))
    project(1, list(range(movers)))
    for copy in home_copies:
        copy.start()
    if movers < holders:
        project(1, list(range(movers, holders)))
    for copy in home_copies:
        copy.wait()
    for k in range(movers):
        for e in range(columns):
            for s in range(PAIR):
                out_ref[PAIR + s, slot(e, k)] = rounded(
                    chosen(e, k, lambda n: home_recv[n, k, s, e])
                )

    def drain(u, carry):
        for e in range(1, columns):
            lat_copy(u, e).wait_send()
            rot_copy(u, e).wait_send()
            back_copy(u, e).wait_send()
        return carry

    lax.fori_loop(0, spans * holders, drain, 0)


def local_part(heads):
    return max(heads // 4, 1)


def body(q_nope, q_rope, w_absorb_k, w_absorb_v, latent_cache, new_latent, lengths, moves):
    steps, slots, heads, width = q_nope.shape
    rope = q_rope.shape[3]
    latent = w_absorb_k.shape[2]
    holders, capacity, entries = latent_cache.shape
    movers = moves.shape[1]
    groups = lax.axis_size("grp")
    columns = lax.axis_size("head")
    scale = YARN_GAIN / math.sqrt(width + rope)
    units = steps // PAIR * holders
    rows = holders * columns * PAIR * heads
    others = groups - 1
    bf16, f32 = jnp.bfloat16, jnp.float32
    dma = pltpu.SemaphoreType.DMA
    vmem = pl.BlockSpec(memory_space=pltpu.VMEM)
    smem = pl.BlockSpec(memory_space=pltpu.SMEM)
    hbm = pl.BlockSpec(memory_space=pl.ANY)
    parts = heads // local_part(heads)
    return pl.pallas_call(
        functools.partial(kernel, groups, columns, scale),
        out_shape=jax.ShapeDtypeStruct(q_nope.shape, bf16),
        in_specs=[smem, smem, vmem, vmem, vmem, hbm, hbm, hbm],
        out_specs=vmem,
        scratch_shapes=[
            pltpu.VMEM(w_absorb_k.shape, bf16),
            pltpu.VMEM(w_absorb_v.shape, bf16),
            pltpu.VMEM((holders, capacity + EXTRA, entries), bf16),
            dma((parts + holders + 1,)),
            pltpu.VMEM((rows, width), f32),
            pltpu.VMEM((latent // LANES, rows, LANES), f32),
            pltpu.VMEM((rows, width), f32),
            pltpu.VMEM((units, columns, PAIR * heads, latent), bf16),
            pltpu.VMEM((units, columns, PAIR * heads, latent), bf16),
            pltpu.VMEM((units, columns, heads, PAIR * rope), bf16),
            pltpu.VMEM((units, columns, heads, PAIR * rope), bf16),
            pltpu.VMEM((units, columns, PAIR * heads, latent), bf16),
            pltpu.VMEM((units, columns, PAIR * heads, latent), bf16),
            pltpu.VMEM((movers, PAIR + 1, columns, heads, width), bf16),
            pltpu.VMEM((others, movers, PAIR + 1, columns, heads, width), bf16),
            pltpu.VMEM((movers, 16, entries), bf16),
            pltpu.VMEM((others, movers, 16, entries), bf16),
            pltpu.VMEM((movers, PAIR, columns, heads, width), bf16),
            pltpu.VMEM((others, movers, PAIR, columns, heads, width), bf16),
            pltpu.VMEM((columns, movers, 8, LANES), jnp.int32),
            pltpu.VMEM((movers, 8, LANES), jnp.int32),
            dma((units, columns)), dma((units, columns)),
            dma((units, columns)), dma((units, columns)),
            dma((units, columns)), dma((units, columns)),
            dma((others,)), dma((others,)),
            dma((others,)), dma((others,)),
            dma((others,)), dma((others,)),
            dma((columns,)), dma((columns,)),
        ],
        compiler_params=pltpu.CompilerParams(
            collective_id=0, has_side_effects=True, vmem_limit_bytes=48 << 20
        ),
    )(lengths, moves, q_nope, q_rope, new_latent, w_absorb_k, w_absorb_v, latent_cache)


def solution(mesh):
    placed = (
        P(None, "grp", "head", None),
        P(None, "grp", "head", None),
        P("head", None, None),
        P("head", None, None),
        P(("grp", "head"), None, None),
        P(None, ("grp", "head"), None),
        P(),
        P("head", None),
    )
    return jax.shard_map(
        body, mesh=mesh, in_specs=placed, out_specs=P(None, "grp", "head", None), check_vma=False
    )
```

time: 187 us -> 77.6 us (0.41)
  Pallas kernels: 0 us -> 72.9 us
  matrix products: 56.6 us -> 0 us
  starting transfers between devices: 42.9 us -> 0 us
  local copies, waits for them, and re-layouts: 35.3 us -> 3.81 us
  waiting for transfers between devices: 26.3 us -> 0 us
  other arithmetic: 22.1 us -> 0 us
  between operations: 3.07 us -> 0.76 us
    pallas_call x0 -> x1, Pallas kernels: none -> 72.9 us  [body(): pl.pallas_call(functools.partial(kernel, groups, columns, scale), out_sha...]
    dot_general x32 -> x0, matrix products: 56.6 us -> none  [the longest x8 18.5 us: score_tile(): jnp.einsum('rhc,rtc->rht', queries, key_rows, preferred_element_type=jnp....]
    all_to_all x8 -> x0, starting transfers between devices: 37.7 us -> none  [the longest x4 20 us: body(): lax.all_to_all(query_rows, 'head', split_axis=0, concat_axis=1, tiled=True)]
    all_to_all x8 -> x0, waiting for transfers between devices: 15.2 us -> none  [the longest x4 12.7 us: body(): lax.all_to_all(latent_out, 'head', split_axis=1, concat_axis=0, tiled=True)]
    while x6 -> x0, local copies, waits for them, and re-layouts: 11.7 us -> none  [attend(): lax.fori_loop(0, passes, value_tile, start_value).astype(jnp.bfloat16)]
    ppermute x6 -> x0, waiting for transfers between devices: 11.1 us -> none  [passed_along(): return lax.ppermute(value, axis, pairs)]
    all_to_all x12 -> x0, local copies, waits for them, and re-layouts: 5.82 us -> none  [the longest x8 3.76 us: body(): lax.all_to_all(latent_out, 'head', split_axis=1, concat_axis=0, tiled=True)]
    select_n x6 -> x0, other arithmetic: 5.64 us -> none  [the longest x3 5.61 us: body(): jnp.where(chosen[:, None, None], arrived[0], moving[0])]
  transfers between devices with their start and end apart: 14 -> 0, of which waited for: 6 -> 0; matrix products, arithmetic and copies ran while one was open for 44% -> 0% of each run, Pallas kernels for 0% -> 0%
where the time goes in v1:
time: 77.6 us; the launch traced here: 77.4 us
  Pallas kernels  72.9 us (94%)
  local copies, waits for them, and re-layouts  3.81 us (5%)
    pallas_call x1, Pallas kernels, body(): pl.pallas_call(functools.partial(kernel, groups, columns, scale), out_sha...  72.9 us
    unnamed x10, local copies, waits for them, and re-layouts  3.81 us

profile of v1, /device:TPU:0, one launch (start us, length us, event | category | flops | bytes accessed | tf_op | source)
XLA Modules:
  0.0 77.4 jit_solution(15268942429586798426)
XLA Ops:
  0.0 0.0 copy-start.3
  0.0 0.0 copy-start.2
  0.0 0.0 copy-start.1
  0.0 0.0 copy-start
  0.7 3.1 %copy.9.cache_hbm = bf16[2,1024,576]{2,1,0:T(8,128)(2,1)S(1)} copy(bf16[2,1024,576]{1,2,0:T(8,128)(2,1)} %param.12) | data formatting | bytes 4718592 | tf_op args[4]
  3.8 0.0 copy-done.3
  3.8 0.0 copy-done.2
  3.8 0.0 copy-done.1
  3.9 0.0 copy-done
  3.9 72.9 %shard_map.82 = bf16[4,8,32,128]{3,2,1,0:T(8,128)(2,1)S(1)} custom-call(s32[64]{0:T(128)S(1)} %copy-done.3, s32[1,1]{1,0:T(1,128)S(6)} %copy.11.move_ref, bf16[4,8,32,128]{3,2,1,0:T(8,128)(2,1)S(1)} %copy-done, bf16[4,8,32,64]{3,2,1,0:T(8,128)(2,1)S(1)} %copy-done.1, bf16[4,2,576]{2,1,0:T(2,128)(2,1)S(1)} %copy-done.2, bf16[32,128,512]{2,1,0:T(8,128)(2,1)} %wk_hbm.1, ...), custom_call_target="tpu_custom_call" | custom-call | tf_op jit(solution)/shard_map/pallas_call | solution.py:344
  76.7 0.7 copy.12
Async XLA Ops:
  0.0 3.8 %copy-start.3 = (s32[64]{0:T(128)S(1)}, s32[64]{0:T(128)}, u32[]{:S(2)}) copy-start(s32[64]{0:T(128)} %length_ref.1) | copy-start | bytes 772
  0.0 3.8 %copy-start.2 = (bf16[4,2,576]{2,1,0:T(2,128)(2,1)S(1)}, bf16[4,2,576]{2,1,0:T(2,128)(2,1)}, u32[]{:S(2)}) copy-start(bf16[4,2,576]{2,1,0:T(2,128)(2,1)} %fresh_ref.1) | copy-start | bytes 27652
  0.0 3.8 %copy-start.1 = (bf16[4,8,32,64]{3,2,1,0:T(8,128)(2,1)S(1)}, bf16[4,8,32,64]{3,2,1,0:T(8,128)(2,1)}, u32[]{:S(2)}) copy-start(bf16[4,8,32,64]{3,2,1,0:T(8,128)(2,1)} %rope_ref.1) | copy-start | bytes 393220
  0.0 3.8 %copy-start = (bf16[4,8,32,128]{3,2,1,0:T(8,128)(2,1)S(1)}, bf16[4,8,32,128]{3,2,1,0:T(8,128)(2,1)}, u32[]{:S(2)}) copy-start(bf16[4,8,32,128]{3,2,1,0:T(8,128)(2,1)} %nope_ref.1) | copy-start | bytes 786436

commit v2 on v1

--- a/solution.py
+++ b/solution.py
@@ -31,7 +31,7 @@
     groups, columns, scale,
     length_ref, move_ref, nope_ref, rope_ref, fresh_ref, wk_hbm, wv_hbm, cache_hbm,
     out_ref,
-    wk, wv, keys, local_sem,
+    wk, wv, keys, newer, local_sem,
     rows_in, rows_mid, rows_out,
     lat_send, lat_recv, rot_send, rot_recv, back_send, back_recv,
     mine, moved, mine_key, moved_key, home, home_recv, shift_of, shift_mine,
@@ -39,12 +39,14 @@
     mine_ss, mine_rs, key_ss, key_rs, home_ss, home_rs, shift_ss, shift_rs,
 ):
     steps, _, heads, _ = nope_ref.shape
-    holders, capacity, entries = cache_hbm.shape
+    holders, entries, capacity = cache_hbm.shape
     latent = wk.shape[2]
     rope = entries - latent
     movers = move_ref.shape[1]
     spans = steps // PAIR
     total = capacity + EXTRA
+    cuts = lat_send.shape[2]
+    cut = heads // cuts
     rank = lax.axis_index("grp")
     column = lax.axis_index("head")
     parts = wk.shape[0] // local_part(heads)
@@ -58,7 +60,7 @@
     ]
     key_copies = [
         pltpu.make_async_copy(
-            cache_hbm.at[k], keys.at[k, pl.ds(0, capacity)], local_sem.at[parts + k]
+            cache_hbm.at[k], keys.at[k], local_sem.at[parts + k]
         )
         for k in range(holders)
     ]
@@ -108,8 +110,8 @@
         return found
 
     for k in range(holders):
-        keys[k, pl.ds(capacity, EXTRA)] = jnp.zeros((EXTRA, entries), jnp.bfloat16)
-        keys[k, pl.ds(capacity, 16)] = rounded(fresh_rows(k))
+        newer[k] = jnp.zeros((EXTRA, entries), jnp.bfloat16)
+        newer[k, 0:16] = rounded(fresh_rows(k))
     for k in range(movers):
         mine_key[k] = rounded(fresh_rows(k))
     pl.semaphore_wait(barrier, columns - 1 + groups - 1)
@@ -132,9 +134,10 @@
         copy.start()
     wv_copy.start()
 
-    def lat_copy(u, e):
+    def lat_copy(u, e, c):
         return remote(
-            lat_send.at[u, e], lat_recv.at[u, e], lat_ss.at[u, e], lat_rs.at[u, e], at_column(e)
+            lat_send.at[u, e, c], lat_recv.at[u, e, c], lat_ss.at[u, e, c], lat_rs.at[u, e, c],
+            at_column(e),
         )
 
     def rot_copy(u, e):
@@ -147,6 +150,16 @@
             back_send.at[u, e], back_recv.at[u, e], back_ss.at[u, e], back_rs.at[u, e],
             at_column(-e),
         )
+
+    low, high = jnp.int32(0), jnp.int32(columns - 1)
+    upward, downward = [], []
+    for _ in range(columns - 1):
+        take_high = high - column >= column - low
+        target = jnp.where(take_high, high, low)
+        upward.append(lax.rem(target - column + columns, columns))
+        downward.append(lax.rem(column - target + columns, columns))
+        high = jnp.where(take_high, high - 1, high)
+        low = jnp.where(take_high, low, low + 1)
 
     def chosen(e, k, options):
         found = wide(options(0))
@@ -160,6 +173,20 @@
 
     def place(k, e, s):
         return ((k * columns + e) * PAIR + s) * heads
+
+    def turn(span, k):
+        u = span * holders + k
+        for e in range(columns):
+            if span and k < movers:
+                pair = rounded(chosen(e, k, lambda n: moved[n, k, PAIR, e]))
+            else:
+                pair = turned(span, e, k)
+            if e:
+                rot_send[u, e] = pair
+            else:
+                rot_recv[u, 0] = pair
+        for e in upward:
+            rot_copy(u, e).start()
 
     def absorb(span, first):
         for k in range(holders):
@@ -170,14 +197,6 @@
                     else:
                         value = wide(nope_ref[span * PAIR + s, slot(e, k)])
                     rows_in[pl.ds(place(k, e, s), heads)] = value
-                if span and k < movers:
-                    pair = rounded(chosen(e, k, lambda n: moved[n, k, PAIR, e]))
-                else:
-                    pair = turned(span, e, k)
-                if e:
-                    rot_send[span * holders + k, e] = pair
-                else:
-                    rot_recv[span * holders + k, 0] = pair
         for n in range(parts):
             if first:
                 wk_copies[n].wait()
@@ -189,45 +208,61 @@
                     rows_mid[c, pl.ds(i, count, stride=heads)] = result[:, lane(c)]
                 return carry
 
-            lax.fori_loop(n * part, (n + 1) * part, head, 0)
-        for k in range(holders):
-            u = span * holders + k
-            for e in range(columns):
-                at = pl.ds(place(k, e, 0), PAIR * heads)
-                value = jnp.concatenate(
-                    [rounded(rows_mid[c, at]) for c in range(latent // LANES)], axis=1
-                )
-                if e:
-                    lat_send[u, e] = value
-                    lat_copy(u, e).start()
-                    rot_copy(u, e).start()
-                else:
-                    lat_recv[u, 0] = value
-
+            lax.fori_loop(n * part, (n + 1) * part, head, 0, unroll=True)
+            if (n + 1) % (parts // cuts):
+                continue
+            c = n // (parts // cuts)
+            for k in range(holders):
+                u = span * holders + k
+                for e in range(columns):
+                    value = jnp.concatenate(
+                        [
+                            jnp.concatenate(
+                                [
+                                    rounded(rows_mid[l, pl.ds(place(k, e, s) + c * cut, cut)])
+                                    for l in range(latent // LANES)
+                                ],
+                                axis=1,
+                            )
+                            for s in range(PAIR)
+                        ],
+                        axis=0,
+                    )
+                    if e:
+                        lat_send[u, e, c] = value
+                    else:
+                        lat_recv[u, 0, c] = value
+                for e in upward:
+                    lat_copy(u, e, c).start()
+
+    for k in range(holders):
+        turn(0, k)
+    for k in range(movers, holders):
+        turn(1, k)
     absorb(0, True)
     for copy in shift_copies:
         copy.wait()
     for copy in mine_copies + newer_copies:
         copy.wait()
-    for span in range(1, spans):
-        absorb(span, False)
+    for k in range(movers):
+        turn(1, k)
+    absorb(1, False)
     for copy in key_copies:
         copy.wait()
     for k in range(movers):
         later = chosen(0, k, lambda n: moved_key[n, k])
-        keys[k, pl.ds(capacity, 16)] = rounded(
-            jnp.where(row < PAIR, wide(keys[k, pl.ds(capacity, 16)]), later)
-        )
+        newer[k, 0:16] = rounded(jnp.where(row < PAIR, wide(newer[k, 0:16]), later))
 
     at_key = lax.broadcasted_iota(jnp.int32, (1, total), 1)
     at_row = lax.broadcasted_iota(jnp.int32, (unit_rows, 1), 0)
-    within = lax.rem(lax.div(at_row, heads), PAIR)
+    within = lax.rem(lax.div(at_row, cut), PAIR)
 
     def unit(u, carry):
         span = lax.div(u, holders)
         k = lax.rem(u, holders)
         for e in range(1, columns):
-            lat_copy(u, e).wait_recv()
+            for c in range(cuts):
+                lat_copy(u, e, c).wait_recv()
             rot_copy(u, e).wait_recv()
         live = length_ref[(rank * columns + column) * holders + k]
         token = jnp.where(at_key < capacity, steps, at_key - capacity)
@@ -236,23 +271,38 @@
         queries = lat_recv[u].reshape(unit_rows, latent)
         turns = rot_recv[u]
         turns = jnp.concatenate(
-            [turns[e][:, s * rope : (s + 1) * rope] for e in range(columns) for s in range(PAIR)],
+            [
+                turns[e][c * cut : (c + 1) * cut, s * rope : (s + 1) * rope]
+                for e in range(columns)
+                for c in range(cuts)
+                for s in range(PAIR)
+            ],
             axis=0,
         )
-        scores = lax.dot_general(
-            queries, keys[k, :, :latent], nt, preferred_element_type=jnp.float32
+        cached = jnp.dot(
+            queries, keys[k, :latent], preferred_element_type=jnp.float32
+        ) + jnp.dot(turns, keys[k, latent:], preferred_element_type=jnp.float32)
+        decoded = lax.dot_general(
+            queries, newer[k, :, :latent], nt, preferred_element_type=jnp.float32
         ) + lax.dot_general(
-            turns, keys[k, :, latent:], nt, preferred_element_type=jnp.float32
-        )
+            turns, newer[k, :, latent:], nt, preferred_element_type=jnp.float32
+        )
+        scores = jnp.concatenate([cached, decoded], axis=1)
         scores = jnp.where(token <= span * PAIR + within, scores * scale, -jnp.inf)
         spread = jnp.exp(scores - jnp.max(scores, axis=1, keepdims=True))
         weights = rounded(spread / jnp.sum(spread, axis=1, keepdims=True))
         mixed = rounded(
-            jnp.dot(weights, keys[k, :, :latent], preferred_element_type=jnp.float32)
+            lax.dot_general(
+                weights[:, :capacity], keys[k, :latent], nt, preferred_element_type=jnp.float32
+            )
+            + jnp.dot(
+                weights[:, capacity:], newer[k, :, :latent], preferred_element_type=jnp.float32
+            )
         ).reshape(columns, PAIR * heads, latent)
         back_recv[u, 0] = mixed[0]
         for e in range(1, columns):
             back_send[u, e] = mixed[e]
+        for e in downward:
             back_copy(u, e).start()
         return carry
 
@@ -267,8 +317,13 @@
                 back_copy(u, e).wait_recv()
             for e in range(columns):
                 value = wide(back_recv[u, e])
-                for c in range(latent // LANES):
-                    rows_mid[c, pl.ds(place(n, e, 0), PAIR * heads)] = value[:, lane(c)]
+                for c in range(cuts):
+                    for s in range(PAIR):
+                        at = (c * PAIR + s) * cut
+                        for l in range(latent // LANES):
+                            rows_mid[l, pl.ds(place(n, e, s) + c * cut, cut)] = value[
+                                at : at + cut, lane(l)
+                            ]
 
         def head(i, carry):
             at = pl.ds(i, held * columns * PAIR, stride=heads)
@@ -280,7 +335,7 @@
             )
             return carry
 
-        lax.fori_loop(0, heads, head, 0)
+        lax.fori_loop(0, heads, head, 0, unroll=min(heads, 8))
         for n, k in enumerate(members):
             for e in range(columns):
                 for s in range(PAIR):
@@ -311,7 +366,8 @@
 
     def drain(u, carry):
         for e in range(1, columns):
-            lat_copy(u, e).wait_send()
+            for c in range(cuts):
+                lat_copy(u, e, c).wait_send()
             rot_copy(u, e).wait_send()
             back_copy(u, e).wait_send()
         return carry
@@ -332,6 +388,7 @@
     groups = lax.axis_size("grp")
     columns = lax.axis_size("head")
     scale = YARN_GAIN / math.sqrt(width + rope)
+    assert steps == 2 * PAIR
     units = steps // PAIR * holders
     rows = holders * columns * PAIR * heads
     others = groups - 1
@@ -341,6 +398,7 @@
     smem = pl.BlockSpec(memory_space=pltpu.SMEM)
     hbm = pl.BlockSpec(memory_space=pl.ANY)
     parts = heads // local_part(heads)
+    cuts = 1 if heads % 32 else 2
     return pl.pallas_call(
         functools.partial(kernel, groups, columns, scale),
         out_shape=jax.ShapeDtypeStruct(q_nope.shape, bf16),
@@ -349,13 +407,14 @@
         scratch_shapes=[
             pltpu.VMEM(w_absorb_k.shape, bf16),
             pltpu.VMEM(w_absorb_v.shape, bf16),
-            pltpu.VMEM((holders, capacity + EXTRA, entries), bf16),
+            pltpu.VMEM((holders, entries, capacity), bf16),
+            pltpu.VMEM((holders, EXTRA, entries), bf16),
             dma((parts + holders + 1,)),
             pltpu.VMEM((rows, width), f32),
             pltpu.VMEM((latent // LANES, rows, LANES), f32),
             pltpu.VMEM((rows, width), f32),
-            pltpu.VMEM((units, columns, PAIR * heads, latent), bf16),
-            pltpu.VMEM((units, columns, PAIR * heads, latent), bf16),
+            pltpu.VMEM((units, columns, cuts, PAIR * heads // cuts, latent), bf16),
+            pltpu.VMEM((units, columns, cuts, PAIR * heads // cuts, latent), bf16),
             pltpu.VMEM((units, columns, heads, PAIR * rope), bf16),
             pltpu.VMEM((units, columns, heads, PAIR * rope), bf16),
             pltpu.VMEM((units, columns, PAIR * heads, latent), bf16),
@@ -368,7 +427,7 @@
             pltpu.VMEM((others, movers, PAIR, columns, heads, width), bf16),
             pltpu.VMEM((columns, movers, 8, LANES), jnp.int32),
             pltpu.VMEM((movers, 8, LANES), jnp.int32),
-            dma((units, columns)), dma((units, columns)),
+            dma((units, columns, cuts)), dma((units, columns, cuts)),
             dma((units, columns)), dma((units, columns)),
             dma((units, columns)), dma((units, columns)),
             dma((others,)), dma((others,)),
@@ -379,7 +438,7 @@
         compiler_params=pltpu.CompilerParams(
             collective_id=0, has_side_effects=True, vmem_limit_bytes=48 << 20
         ),
-    )(lengths, moves, q_nope, q_rope, new_latent, w_absorb_k, w_absorb_v, latent_cache)
+    )(lengths, moves, q_nope, q_rope, new_latent, w_absorb_k, w_absorb_v, jnp.swapaxes(latent_cache, 1, 2))
 
 
 def solution(mesh):

time: 77.6 us -> 68.4 us (0.88)
  Pallas kernels: 72.9 us -> 61.8 us
  local copies, waits for them, and re-layouts: 3.81 us -> 5.62 us
    pallas_call x1, Pallas kernels: 72.9 us -> 61.8 us  [body(): pl.pallas_call(functools.partial(kernel, groups, columns, scale), out_sha...]
    unnamed x10 -> x11, local copies, waits for them, and re-layouts: 3.81 us -> 5.62 us
where the time goes in v2:
time: 68.4 us; the launch traced here: 68.1 us
  Pallas kernels  61.8 us (90%)
  local copies, waits for them, and re-layouts  5.62 us (8%)
    pallas_call x1, Pallas kernels, body(): pl.pallas_call(functools.partial(kernel, groups, columns, scale), out_sha...  61.8 us
    unnamed x11, local copies, waits for them, and re-layouts  5.62 us

profile of v2, /device:TPU:0, one launch (start us, length us, event | category | flops | bytes accessed | tf_op | source)
XLA Modules:
  0.0 68.1 jit_solution(13138214838758460619)
XLA Ops:
  0.7 0.0 copy-start
  0.7 1.7 %copy-done = bf16[2,1024,576]{1,2,0:T(8,128)(2,1)S(1)} copy-done((bf16[2,1024,576]{1,2,0:T(8,128)(2,1)S(1)}, bf16[2,1024,576]{1,2,0:T(8,128)(2,1)}, u32[]{:S(2)}) %copy-start) | copy-done | bytes 2359320
  2.3 0.0 copy-start.1
  2.3 0.9 %copy-done.1 = bf16[4,8,32,128]{3,2,1,0:T(8,128)(2,1)S(1)} copy-done((bf16[4,8,32,128]{3,2,1,0:T(8,128)(2,1)S(1)}, bf16[4,8,32,128]{3,2,1,0:T(8,128)(2,1)}, u32[]{:S(2)}) %copy-start.1) | copy-done | bytes 262168
  3.3 0.0 copy-start.2
  3.3 0.9 %copy-done.2 = bf16[4,8,32,64]{3,2,1,0:T(8,128)(2,1)S(1)} copy-done((bf16[4,8,32,64]{3,2,1,0:T(8,128)(2,1)S(1)}, bf16[4,8,32,64]{3,2,1,0:T(8,128)(2,1)}, u32[]{:S(2)}) %copy-start.2) | copy-done | bytes 131096
  4.2 0.0 copy-start.3
  4.2 0.7 %copy-done.3 = bf16[4,2,576]{2,1,0:T(2,128)(2,1)S(1)} copy-done((bf16[4,2,576]{2,1,0:T(2,128)(2,1)S(1)}, bf16[4,2,576]{2,1,0:T(2,128)(2,1)}, u32[]{:S(2)}) %copy-start.3) | copy-done | bytes 9240
  4.9 0.0 copy-start.4
  4.9 0.7 copy-done.4
  5.6 61.8 %shard_map.82 = bf16[4,8,32,128]{3,2,1,0:T(8,128)(2,1)S(1)} custom-call(s32[64]{0:T(128)S(1)} %copy-done.4, s32[1,1]{1,0:T(1,128)S(6)} %copy.10.move_ref, bf16[4,8,32,128]{3,2,1,0:T(8,128)(2,1)S(1)} %copy-done.1, bf16[4,8,32,64]{3,2,1,0:T(8,128)(2,1)S(1)} %copy-done.2, bf16[4,2,576]{2,1,0:T(2,128)(2,1)S(1)} %copy-done.3, bf16[32,128,512]{2,1,0:T(8,128)(2,1)} %wk_hbm.1, ...), custom_call_target="tpu_custom_call" | custom-call | tf_op jit(solution)/shard_map/pallas_call | solution.py:402
  67.4 0.7 %copy.11 = bf16[4,8,32,128]{3,2,1,0:T(8,128)(2,1)} copy(bf16[4,8,32,128]{3,2,1,0:T(8,128)(2,1)S(1)} %shard_map.82) | data formatting | bytes 524288
Async XLA Ops:
  0.7 1.7 %copy-start = (bf16[2,1024,576]{1,2,0:T(8,128)(2,1)S(1)}, bf16[2,1024,576]{1,2,0:T(8,128)(2,1)}, u32[]{:S(2)}) copy-start(bf16[2,1024,576]{1,2,0:T(8,128)(2,1)} %param.12) | copy-start | bytes 7077892
  2.3 0.9 %copy-start.1 = (bf16[4,8,32,128]{3,2,1,0:T(8,128)(2,1)S(1)}, bf16[4,8,32,128]{3,2,1,0:T(8,128)(2,1)}, u32[]{:S(2)}) copy-start(bf16[4,8,32,128]{3,2,1,0:T(8,128)(2,1)} %nope_ref.1) | copy-start | bytes 786436
  3.3 0.9 %copy-start.2 = (bf16[4,8,32,64]{3,2,1,0:T(8,128)(2,1)S(1)}, bf16[4,8,32,64]{3,2,1,0:T(8,128)(2,1)}, u32[]{:S(2)}) copy-start(bf16[4,8,32,64]{3,2,1,0:T(8,128)(2,1)} %rope_ref.1) | copy-start | bytes 393220
  4.2 0.7 %copy-start.3 = (bf16[4,2,576]{2,1,0:T(2,128)(2,1)S(1)}, bf16[4,2,576]{2,1,0:T(2,128)(2,1)}, u32[]{:S(2)}) copy-start(bf16[4,2,576]{2,1,0:T(2,128)(2,1)} %fresh_ref.1) | copy-start | bytes 27652
  4.9 0.7 copy-start.4

commit v3 on v2

--- a/solution.py
+++ b/solution.py
@@ -29,8 +29,9 @@
 
 def kernel(
     groups, columns, scale,
-    length_ref, move_ref, nope_ref, rope_ref, fresh_ref, wk_hbm, wv_hbm, cache_hbm,
+    length_ref, move_ref, nope_hbm, rope_hbm, fresh_hbm, wk_hbm, wv_hbm, cache_hbm,
     out_ref,
+    nope_ref, rope_ref, fresh_ref, entry_sem,
     wk, wv, keys, newer, local_sem,
     rows_in, rows_mid, rows_out,
     lat_send, lat_recv, rot_send, rot_recv, back_send, back_recv,
@@ -65,7 +66,13 @@
         for k in range(holders)
     ]
     wv_copy = pltpu.make_async_copy(wv_hbm, wv, local_sem.at[parts + holders])
-    for copy in wk_copies:
+    entry_copies = [
+        pltpu.make_async_copy(src, dst, entry_sem.at[n])
+        for n, (src, dst) in enumerate(
+            ((rope_hbm, rope_ref), (nope_hbm, nope_ref), (fresh_hbm, fresh_ref))
+        )
+    ]
+    for copy in entry_copies + wk_copies:
         copy.start()
 
     def at_column(e):
@@ -94,6 +101,8 @@
             [rope_ref[span * PAIR + s, slot(e, k)] for s in range(PAIR)], axis=1
         )
 
+    for copy in entry_copies:
+        copy.wait()
     for k in range(movers):
         for e in range(columns):
             for s in range(PAIR):
@@ -130,9 +139,6 @@
     ]
     for copy in shift_copies + mine_copies + newer_copies:
         copy.start()
-    for copy in key_copies:
-        copy.start()
-    wv_copy.start()
 
     def lat_copy(u, e, c):
         return remote(
@@ -168,7 +174,6 @@
             found = jnp.where(is_it, wide(options(d - 1)), found)
         return found
 
-    count = holders * columns * PAIR
     unit_rows = columns * PAIR * heads
 
     def place(k, e, s):
@@ -188,15 +193,16 @@
         for e in upward:
             rot_copy(u, e).start()
 
-    def absorb(span, first):
-        for k in range(holders):
+    def absorb(members, first):
+        count = len(members) * columns * PAIR
+        for m, (span, k) in enumerate(members):
             for e in range(columns):
                 for s in range(PAIR):
                     if span and k < movers:
                         value = chosen(e, k, lambda n: moved[n, k, s, e])
                     else:
                         value = wide(nope_ref[span * PAIR + s, slot(e, k)])
-                    rows_in[pl.ds(place(k, e, s), heads)] = value
+                    rows_in[pl.ds(place(m, e, s), heads)] = value
         for n in range(parts):
             if first:
                 wk_copies[n].wait()
@@ -212,14 +218,14 @@
             if (n + 1) % (parts // cuts):
                 continue
             c = n // (parts // cuts)
-            for k in range(holders):
+            for m, (span, k) in enumerate(members):
                 u = span * holders + k
                 for e in range(columns):
                     value = jnp.concatenate(
                         [
                             jnp.concatenate(
                                 [
-                                    rounded(rows_mid[l, pl.ds(place(k, e, s) + c * cut, cut)])
+                                    rounded(rows_mid[l, pl.ds(place(m, e, s) + c * cut, cut)])
                                     for l in range(latent // LANES)
                                 ],
                                 axis=1,
@@ -235,18 +241,21 @@
                 for e in upward:
                     lat_copy(u, e, c).start()
 
-    for k in range(holders):
-        turn(0, k)
-    for k in range(movers, holders):
-        turn(1, k)
-    absorb(0, True)
+    settled = [(0, k) for k in range(holders)] + [(1, k) for k in range(movers, holders)]
+    moving = [(1, k) for k in range(movers)]
+    for span, k in settled:
+        turn(span, k)
+    absorb(settled, True)
+    for copy in key_copies:
+        copy.start()
     for copy in shift_copies:
         copy.wait()
     for copy in mine_copies + newer_copies:
         copy.wait()
-    for k in range(movers):
-        turn(1, k)
-    absorb(1, False)
+    for span, k in moving:
+        turn(span, k)
+    absorb(moving, False)
+    wv_copy.start()
     for copy in key_copies:
         copy.wait()
     for k in range(movers):
@@ -390,7 +399,7 @@
     scale = YARN_GAIN / math.sqrt(width + rope)
     assert steps == 2 * PAIR
     units = steps // PAIR * holders
-    rows = holders * columns * PAIR * heads
+    rows = (2 * holders - movers) * columns * PAIR * heads
     others = groups - 1
     bf16, f32 = jnp.bfloat16, jnp.float32
     dma = pltpu.SemaphoreType.DMA
@@ -402,9 +411,13 @@
     return pl.pallas_call(
         functools.partial(kernel, groups, columns, scale),
         out_shape=jax.ShapeDtypeStruct(q_nope.shape, bf16),
-        in_specs=[smem, smem, vmem, vmem, vmem, hbm, hbm, hbm],
+        in_specs=[smem, smem, hbm, hbm, hbm, hbm, hbm, hbm],
         out_specs=vmem,
         scratch_shapes=[
+            pltpu.VMEM(q_nope.shape, bf16),
+            pltpu.VMEM(q_rope.shape, bf16),
+            pltpu.VMEM(new_latent.shape, bf16),
+            dma((3,)),
             pltpu.VMEM(w_absorb_k.shape, bf16),
             pltpu.VMEM(w_absorb_v.shape, bf16),
             pltpu.VMEM((holders, entries, capacity), bf16),
@@ -436,7 +449,7 @@
             dma((columns,)), dma((columns,)),
         ],
         compiler_params=pltpu.CompilerParams(
-            collective_id=0, has_side_effects=True, vmem_limit_bytes=48 << 20
+            collective_id=0, has_side_effects=True, vmem_limit_bytes=60 << 20
         ),
     )(lengths, moves, q_nope, q_rope, new_latent, w_absorb_k, w_absorb_v, jnp.swapaxes(latent_cache, 1, 2))
 

time: 68.4 us -> 65 us (0.950)
  local copies, waits for them, and re-layouts: 5.62 us -> 1.67 us
  Pallas kernels: 61.8 us -> 62.5 us
    unnamed x11 -> x1, local copies, waits for them, and re-layouts: 5.62 us -> 1.67 us
where the time goes in v3:
time: 65 us; the launch traced here: 64.8 us
  Pallas kernels  62.5 us (96%)
  local copies, waits for them, and re-layouts  1.67 us (3%)
  between operations  0.66 us (1%)
    pallas_call x1, Pallas kernels, body(): pl.pallas_call(functools.partial(kernel, groups, columns, scale), out_sha...  62.5 us
    unnamed x1, local copies, waits for them, and re-layouts  1.67 us

profile of v3, /device:TPU:0, one launch (start us, length us, event | category | flops | bytes accessed | tf_op | source)
XLA Modules:
  0.0 64.8 jit_solution(18040112571983525230)
XLA Ops:
  0.7 62.5 %shard_map.82 = bf16[4,8,32,128]{3,2,1,0:T(8,128)(2,1)} custom-call(s32[64]{0:T(128)} %length_ref.1, s32[1,1]{1,0:T(1,128)S(6)} %copy.10.move_ref, bf16[4,8,32,128]{3,2,1,0:T(8,128)(2,1)} %nope_hbm.1, bf16[4,8,32,64]{3,2,1,0:T(8,128)(2,1)} %rope_hbm.1, bf16[4,2,576]{2,1,0:T(2,128)(2,1)} %fresh_hbm.1, bf16[32,128,512]{2,1,0:T(8,128)(2,1)} %wk_hbm.1, ...), custom_call_target="tpu_custom_call" | custom-call | tf_op jit(solution)/shard_map/pallas_call | solution.py:411
  63.1 1.7 %copy.11 = bf16[4,8,32,128]{3,2,1,0:T(8,128)(2,1)} copy(bf16[4,8,32,128]{3,2,1,0:T(8,128)(2,1)} %shard_map.82) | data formatting | bytes 524288
